TPU v7x, 32 devices: a whole 2x2x4 slice. The times are simulated.
32 devices in a mesh: grp: 8 (over y, x, core), cli: 4 (over z).
Axes of the slice: x: 2, y: 2, z: 4, core: 2. Of those that a mesh axis runs over, the one named last changes fastest.
Arguments:
- token_ids: int32 [32, 128], P(('grp', 'cli')), may hold values from 0 to 51199
- target_ids: int32 [32, 128], P(('grp', 'cli')), may hold values from 0 to 51199
- segment_ids: int32 [32, 128], P(('grp', 'cli')), may hold values from 0 to 3, never falling along the last dimension, each value on 1 to 64 neighbouring positions
- chosen: int32 [32], P(('grp', 'cli')), may hold values from 0 to 3, as said below
- table: float32 [4, 51200, 768], P(None, ('grp', 'cli')), may hold values from -0.4375 to 0.4375
- table_momentum: float32 [4, 51200, 768], P(None, ('grp', 'cli')), may hold values from -0.00390625 to 0.00390625
- stack: float32 [4, 9344, 768], P(None, ('grp', 'cli')), may hold values from -0.21875 to 0.21875
- stack_momentum: float32 [4, 9344, 768], P(None, ('grp', 'cli')), may hold values from -0.009765625 to 0.009765625
- vectors: float32 [4, 14, 768], replicated, may hold values from -1 to 1.4
- vector_momentum: float32 [4, 14, 768], replicated, may hold values from -0.0546875 to 0.0546875
Outputs:
- loss: float32 [], replicated
- client_losses: float32 [32, 4], P(('grp', 'cli'))
- table_grad: float32 [4, 51200, 768], P(None, ('grp', 'cli'))
- table_momentum_new: float32 [4, 51200, 768], P(None, ('grp', 'cli'))
- table_new: float32 [4, 51200, 768], P(None, ('grp', 'cli'))
- stack_grad: float32 [4, 9344, 768], P(None, ('grp', 'cli'))
- stack_momentum_new: float32 [4, 9344, 768], P(None, ('grp', 'cli'))
- stack_new: float32 [4, 9344, 768], P(None, ('grp', 'cli'))
- vector_grad: float32 [4, 14, 768], replicated
- vector_momentum_new: float32 [4, 14, 768], replicated
- vector_new: float32 [4, 14, 768], replicated
Inputs may be any that keep to these rules, and one draw needn't show every extreme that they name: Every one of the 4 models is chosen by at least one client.
All inputs are finite; a program needn't handle non-finite values.
Results may differ from a plain program's by a relative error of at most 0.0095.
Values may be sent and summed in bfloat16 or wider, within the bound.
A program may use at most 1 GiB of HBM per device.

v0:
```python
import jax
import jax.numpy as jnp
from jax import lax
from jax.sharding import PartitionSpec as P

HEADS = 12
HEAD_DIM = 64
epsilon = 1e-05
momentum_decay = 0.9
table_rate = 4.0
stack_rate = 4.0
vector_rate = 50.0


def layer_norm(inputs, gain_row, shift_row):
    centred = inputs - jnp.mean(inputs, -1, keepdims=True)
    spread = jnp.mean(centred * centred, -1, keepdims=True)
    return centred * lax.rsqrt(spread + epsilon) * gain_row + shift_row


def project(inputs, matrix):
    return lax.dot_general(
        inputs, matrix, (((1,), (1,)), ((), ())), preferred_element_type=jnp.float32
    )


def product(inputs, matrix):
    return jnp.dot(inputs, matrix, preferred_element_type=jnp.float32)


def outer_rows(left, right):
    return lax.dot_general(
        left, right, (((0,), (0,)), ((), ())), preferred_element_type=jnp.float32
    )


def attend(queries, key_rows, segment_row):
    row_count = queries.shape[0]
    head_shape = (row_count, HEADS, HEAD_DIM)
    scores = jnp.einsum(
        "qhd,khd->hqk",
        queries.reshape(head_shape),
        key_rows.reshape(head_shape),
        preferred_element_type=jnp.float32,
    ) * HEAD_DIM ** (-0.5)
    positions = jnp.arange(row_count)
    allowed = (positions[None, :] <= positions[:, None]) & (
        segment_row[None, :] == segment_row[:, None]
    )
    return jax.nn.softmax(jnp.where(allowed[None], scores, -1e30), axis=-1)


def layer_forward(weights, vector_one, inputs, segment_row):
    model_width = inputs.shape[1]
    row_count = inputs.shape[0]
    normed = layer_norm(inputs, vector_one[0], vector_one[1]).astype(jnp.bfloat16)
    queries = (project(normed, weights[0:model_width]) + vector_one[6]).astype(jnp.bfloat16)
    key_rows = project(normed, weights[model_width : 2 * model_width]).astype(jnp.bfloat16)
    values = (project(normed, weights[2 * model_width : 3 * model_width]) + vector_one[7]).astype(
        jnp.bfloat16
    )
    attention = attend(queries, key_rows, segment_row)
    head_shape = (row_count, HEADS, HEAD_DIM)
    mixture = jnp.einsum(
        "hqk,khd->qhd",
        attention.astype(jnp.bfloat16),
        values.reshape(head_shape),
        preferred_element_type=jnp.float32,
    )
    mixture = mixture.reshape(row_count, model_width).astype(jnp.bfloat16)
    middle = inputs + (project(mixture, weights[3 * model_width : 4 * model_width]) + vector_one[8])
    normed_two = layer_norm(middle, vector_one[2], vector_one[3]).astype(jnp.bfloat16)
    hidden = project(normed_two, weights[4 * model_width : 8 * model_width]) + vector_one[
        10:14
    ].reshape(-1)
    active = jax.nn.gelu(hidden, approximate=True).astype(jnp.bfloat16)
    residual = middle + (
        product(active, weights[8 * model_width : 12 * model_width]) + vector_one[9]
    )
    normed_out = layer_norm(residual, vector_one[4], vector_one[5]).astype(jnp.bfloat16)
    return (
        normed,
        queries,
        key_rows,
        values,
        attention,
        mixture,
        middle,
        normed_two,
        hidden,
        active,
        residual,
        normed_out,
    )


def norm_grad(operand, gain_row, shift_row, cotangent):
    outcome, pullback = jax.vjp(layer_norm, operand, gain_row, shift_row)
    return pullback(cotangent)


def gelu_tanh(hidden):
    return jax.nn.gelu(hidden, approximate=True)


def layer_backward(weights, vector_one, inputs, segment_row, grad_out):
    model_width = inputs.shape[1]
    row_count = inputs.shape[0]
    head_shape = (row_count, HEADS, HEAD_DIM)
    scaling = HEAD_DIM ** (-0.5)
    (
        normed,
        queries,
        key_rows,
        values,
        attention,
        mixture,
        middle,
        normed_two,
        hidden,
        active,
        residual,
        normed_out,
    ) = layer_forward(weights, vector_one, inputs, segment_row)
    d_residual, d_gain_out, d_shift_out = norm_grad(
        residual, vector_one[4], vector_one[5], grad_out
    )
    d_outer = d_residual.astype(jnp.bfloat16)
    d_bias_out = jnp.sum(d_outer.astype(jnp.float32), 0)
    grad_down = outer_rows(active, d_outer)
    d_active = project(d_outer, weights[8 * model_width : 12 * model_width])
    gelu_value, gelu_pull = jax.vjp(gelu_tanh, hidden)
    d_hidden = gelu_pull(d_active)[0].astype(jnp.bfloat16)
    d_bias_hidden = jnp.sum(d_hidden.astype(jnp.float32), 0)
    grad_up = outer_rows(d_hidden, normed_two)
    d_normed_two = product(d_hidden, weights[4 * model_width : 8 * model_width])
    d_middle_norm, d_gain_two, d_shift_two = norm_grad(
        middle, vector_one[2], vector_one[3], d_normed_two
    )
    d_middle = d_residual + d_middle_norm
    d_branch = d_middle.astype(jnp.bfloat16)
    d_bias_branch = jnp.sum(d_branch.astype(jnp.float32), 0)
    grad_mix = outer_rows(d_branch, mixture)
    d_mixture = (
        product(d_branch, weights[3 * model_width : 4 * model_width])
        .astype(jnp.bfloat16)
        .reshape(head_shape)
    )
    d_attention = jnp.einsum(
        "qhd,khd->hqk", d_mixture, values.reshape(head_shape), preferred_element_type=jnp.float32
    )
    d_values = jnp.einsum(
        "hqk,qhd->khd",
        attention.astype(jnp.bfloat16),
        d_mixture,
        preferred_element_type=jnp.float32,
    )
    d_values = d_values.reshape(row_count, model_width).astype(jnp.bfloat16)
    d_scores = (
        attention * (d_attention - jnp.sum(attention * d_attention, -1, keepdims=True))
    ).astype(jnp.bfloat16)
    d_queries = (
        jnp.einsum(
            "hqk,khd->qhd",
            d_scores,
            key_rows.reshape(head_shape),
            preferred_element_type=jnp.float32,
        )
        * scaling
    )
    d_queries = d_queries.reshape(row_count, model_width).astype(jnp.bfloat16)
    d_keys = (
        jnp.einsum(
            "hqk,qhd->khd",
            d_scores,
            queries.reshape(head_shape),
            preferred_element_type=jnp.float32,
        )
        * scaling
    )
    d_keys = d_keys.reshape(row_count, model_width).astype(jnp.bfloat16)
    d_joined = jnp.concatenate([d_queries, d_keys, d_values], axis=1)
    grad_joined = outer_rows(d_joined, normed)
    d_normed = product(d_joined, weights[0 : 3 * model_width])
    d_inputs_norm, d_gain_one, d_shift_one = norm_grad(
        inputs, vector_one[0], vector_one[1], d_normed
    )
    d_inputs = d_middle + d_inputs_norm
    stack_rows = jnp.concatenate([grad_joined, grad_mix, grad_up, grad_down, d_inputs], axis=0)
    bias_query = jnp.sum(d_queries.astype(jnp.float32), 0)
    bias_value = jnp.sum(d_values.astype(jnp.float32), 0)
    vector_rows = jnp.concatenate(
        [
            jnp.stack(
                [
                    d_gain_one,
                    d_shift_one,
                    d_gain_two,
                    d_shift_two,
                    d_gain_out,
                    d_shift_out,
                    bias_query,
                    bias_value,
                    d_bias_branch,
                    d_bias_out,
                ]
            ),
            d_bias_hidden.reshape(4, model_width),
        ],
        axis=0,
    )
    return (stack_rows, vector_rows, d_inputs)


def update(weight, momentum, gradient, step_rate):
    renewed = momentum_decay * momentum + gradient
    return (renewed, weight - step_rate * (gradient + momentum_decay * renewed))


def body(
    token_ids,
    target_ids,
    segment_ids,
    chosen,
    table,
    table_momentum,
    stack,
    stack_momentum,
    vectors,
    vector_momentum,
):
    models = table.shape[0]
    block_rows = table.shape[1]
    model_width = table.shape[2]
    seq_len = token_ids.shape[1]
    devices = lax.axis_size(("grp", "cli"))
    group_size = lax.axis_size("cli")
    device_index = lax.axis_index(("grp", "cli"))
    member_index = lax.axis_index("cli")
    token_row = token_ids[0]
    target_row = target_ids[0]
    segment_row = segment_ids[0]
    model_index = chosen[0]
    model_range = jnp.arange(models, dtype=jnp.int32)
    valid_row = jnp.concatenate(
        [(segment_row[:-1] == segment_row[1:]).astype(jnp.float32), jnp.zeros((1,), jnp.float32)]
    )
    count_own = jnp.sum(valid_row)
    own_choice = (model_range == model_index).astype(jnp.float32)
    client_rows = jnp.where(
        (jnp.arange(devices) == device_index)[:, None], (own_choice * count_own)[None, :], 0.0
    )
    client_rows = lax.psum(client_rows, ("grp", "cli"))
    totals = jnp.sum(client_rows, axis=0)
    model_column = jnp.full((seq_len,), model_index, jnp.int32)
    group_tokens, group_targets, group_valid, group_models = (
        lax.all_gather(token_row, "cli", axis=0, tiled=True),
        lax.all_gather(target_row, "cli", axis=0, tiled=True),
        lax.all_gather(valid_row.astype(jnp.int32), "cli", axis=0, tiled=True),
        lax.all_gather(model_column, "cli", axis=0, tiled=True),
    )
    stack_all = lax.all_gather(stack.astype(jnp.bfloat16), ("grp", "cli"), axis=1, tiled=True)
    table_part = lax.all_gather(table.astype(jnp.bfloat16), "grp", axis=1, tiled=True)
    part_rows = table_part.shape[1]

    def locate(global_ids):
        block_index = global_ids // block_rows
        is_owned = block_index % group_size == member_index
        local_rows = jnp.where(
            is_owned, block_index // group_size * block_rows + global_ids % block_rows, 0
        )
        return (is_owned, local_rows)

    token_owned, token_local = locate(group_tokens)
    target_owned, target_local = locate(group_targets)
    picked = jnp.take(table_part, token_local, axis=1)
    embed_terms = jnp.where(token_owned[None, :, None], picked, jnp.zeros_like(picked)).astype(
        jnp.float32
    )
    embedded = lax.psum_scatter(
        embed_terms.astype(jnp.bfloat16), "cli", scatter_dimension=1, tiled=True
    ).astype(jnp.float32)
    inputs = embedded + stack_all[:, 12 * model_width :, :].astype(jnp.float32)

    def forward_one(element):
        return layer_forward(element[0], element[1], element[2], segment_row)[11]

    normed_outs = lax.map(forward_one, (stack_all, vectors, inputs))
    group_outs = lax.all_gather(normed_outs, "cli", axis=1, tiled=True)

    def head_stats(element):
        outs_one, table_one = element
        logits = project(outs_one, table_one)
        highest = jnp.max(logits, -1)
        exp_total = jnp.sum(jnp.exp(logits - highest[:, None]), -1)
        target_logit = jnp.where(
            target_owned, jnp.take_along_axis(logits, target_local[:, None], axis=1)[:, 0], 0.0
        )
        return (highest, exp_total, target_logit)

    highests, exp_totals, target_logits = lax.map(head_stats, (group_outs, table_part))
    highest_all = lax.pmax(highests, "cli")
    sum_all, target_all = (
        lax.psum((exp_totals * jnp.exp(highests - highest_all)).astype(jnp.bfloat16), "cli").astype(
            jnp.float32
        ),
        lax.psum(target_logits.astype(jnp.bfloat16), "cli").astype(jnp.float32),
    )
    log_totals = highest_all + jnp.log(sum_all)
    token_loss = log_totals - target_all
    own_loss = lax.dynamic_slice_in_dim(token_loss, member_index * seq_len, seq_len, 1)
    client_losses = (jnp.sum(own_loss * valid_row[None, :], axis=1) / count_own)[None, :]
    own_total = jnp.sum(own_choice * totals)
    loss_term = jnp.sum(jnp.sum(own_loss * own_choice[:, None], 0) * valid_row) / own_total
    group_totals = jnp.sum(
        jnp.where(group_models[:, None] == model_range[None, :], totals[None, :], 0.0), axis=1
    )
    token_weight = group_valid.astype(jnp.float32) / group_totals
    vocab_range = jnp.arange(part_rows)

    def head_back(grad_table, block_index):
        block_start = block_index * seq_len
        model_pick = group_models[block_start]
        outs_block = lax.dynamic_slice(
            group_outs, (model_pick, block_start, 0), (1, seq_len, model_width)
        )[0]
        table_one = lax.dynamic_index_in_dim(table_part, model_pick, 0, keepdims=False)
        logits = project(outs_block, table_one)
        lse_block = lax.dynamic_slice(log_totals, (model_pick, block_start), (1, seq_len))[0]
        softmax_rows = jnp.exp(logits - lse_block[:, None])
        target_block = lax.dynamic_slice_in_dim(target_local, block_start, seq_len)
        owned_block = lax.dynamic_slice_in_dim(target_owned, block_start, seq_len)
        weight_block = lax.dynamic_slice_in_dim(token_weight, block_start, seq_len)
        target_hit = (
            (vocab_range[None, :] == target_block[:, None]) & owned_block[:, None]
        ).astype(jnp.float32)
        d_logits = (weight_block[:, None] * (softmax_rows - target_hit)).astype(jnp.bfloat16)
        d_outs = product(d_logits, table_one)
        grad_rows = outer_rows(d_logits, outs_block)
        current = lax.dynamic_index_in_dim(grad_table, model_pick, 0, keepdims=False)
        grad_table = lax.dynamic_update_index_in_dim(grad_table, current + grad_rows, model_pick, 0)
        return (grad_table, d_outs)

    head_init = jnp.zeros((models, part_rows, model_width), jnp.float32)
    grad_table, d_outs = lax.scan(head_back, head_init, jnp.arange(group_size))
    d_final = lax.psum_scatter(
        d_outs.reshape(group_size * seq_len, model_width), "cli", scatter_dimension=0, tiled=True
    )
    stack_one = lax.dynamic_index_in_dim(stack_all, model_index, 0, keepdims=False)
    vector_one = lax.dynamic_index_in_dim(vectors, model_index, 0, keepdims=False)
    inputs_one = lax.dynamic_index_in_dim(inputs, model_index, 0, keepdims=False)
    stack_rows, vector_rows, d_inputs = layer_backward(
        stack_one, vector_one, inputs_one, segment_row, d_final
    )
    group_grads = lax.all_gather(d_inputs.astype(jnp.bfloat16), "cli", axis=0, tiled=True)
    drop_rows = jnp.where(token_owned, token_local, part_rows)
    grad_table = grad_table.at[group_models, drop_rows].add(
        group_grads.astype(jnp.float32), mode="drop"
    )
    table_grad = lax.psum_scatter(
        grad_table.astype(jnp.bfloat16), "grp", scatter_dimension=1, tiled=True
    ).astype(jnp.float32)
    masked = jnp.where((model_range == model_index)[:, None, None], stack_rows[None], 0.0)
    stack_grad = lax.psum_scatter(masked, ("grp", "cli"), scatter_dimension=1, tiled=True)
    vector_masked = jnp.where((model_range == model_index)[:, None, None], vector_rows[None], 0.0)
    vector_grad, loss = lax.psum((vector_masked, loss_term), ("grp", "cli"))
    table_momentum_new, table_new = update(table, table_momentum, table_grad, table_rate)
    stack_momentum_new, stack_new = update(stack, stack_momentum, stack_grad, stack_rate)
    vector_momentum_new, vector_new = update(vectors, vector_momentum, vector_grad, vector_rate)
    return (
        loss,
        client_losses,
        table_grad,
        table_momentum_new,
        table_new,
        stack_grad,
        stack_momentum_new,
        stack_new,
        vector_grad,
        vector_momentum_new,
        vector_new,
    )


def solution(mesh):
    placed = (
        P(("grp", "cli"), None),
        P(("grp", "cli"), None),
        P(("grp", "cli"), None),
        P(("grp", "cli")),
        P(None, ("grp", "cli"), None),
        P(None, ("grp", "cli"), None),
        P(None, ("grp", "cli"), None),
        P(None, ("grp", "cli"), None),
        P(),
        P(),
    )
    return jax.shard_map(
        body,
        mesh=mesh,
        in_specs=placed,
        out_specs=(
            P(),
            P(("grp", "cli"), None),
            P(None, ("grp", "cli"), None),
            P(None, ("grp", "cli"), None),
            P(None, ("grp", "cli"), None),
            P(None, ("grp", "cli"), None),
            P(None, ("grp", "cli"), None),
            P(None, ("grp", "cli"), None),
            P(),
            P(),
            P(),
        ),
        check_vma=False,
    )
```

profile of v0, /device:TPU:0, one launch (start us, length us, event | category | flops | bytes accessed | tf_op | source)
XLA Modules:
  0.0 3884.0 jit_solution(11815534252745579856)
XLA Ops:
  7.2 29.7 copy.117
  54.1 338.0 %all-gather.8.cloned.1.call-done = bf16[4,12800,768]{2,0,1:T(4,128)(2,1)} async-done(((bf16[4,1600,768]{2,0,1:T(4,128)(2,1)}), bf16[4,12800,768]{2,0,1:T(4,128)(2,1)}) %all-gather.8.cloned.1.call-update) | async-done | bytes 78643216 | tf_op jit(solution)/shard_map/all_gather | solution.py:263
  392.1 17.6 gather_fusion.1
  415.7 289.6 %all-gather.10.cloned.1.call-done = bf16[4,9344,768]{2,0,1:T(4,128)(2,1)} async-done(((bf16[4,292,768]{2,0,1:T(4,128)(2,1)}), bf16[4,9344,768]{2,0,1:T(4,128)(2,1)}) %all-gather.10.cloned.1.call-update) | async-done | bytes 57409552 | tf_op jit(solution)/shard_map/all_gather | solution.py:262
  705.3 38.5 copy.97
  743.9 83.7 %all-reduce.9.cloned.1.call-done = bf16[4,512,768]{2,0,1:T(4,128)(2,1)} async-done(((bf16[4,512,768]{2,0,1:T(4,128)(2,1)}), bf16[4,512,768]{2,0,1:T(4,128)(2,1)}) %all-reduce.9.cloned.1.call-update) | async-done | bytes 3145744
  830.3 68.9 %while.37 = (s32[]{:T(128)}, bf16[4,128,768]{2,1,0:T(8,128)(2,1)}, f32[4,128,768]{2,1,0:T(8,128)S(1)}, f32[4,14,768]{2,0,1:T(4,128)S(1)}, bf16[4,9344,768]{2,1,0...) while((s32[]{:T(128)}, bf16[4,128,768]{2,1,0:T(8,128)(2,1)}, ...), condition=%wide.region_10.11_spmd, body=%wide.region_1.10_spmd.sunk | while | flops 1896827008 | bytes 24394716 | solution.py:288
  901.4 42.1 %psum.37 = f32[32,4]{0,1:T(4,128)S(1)} all-reduce(f32[32,4]{0,1:T(4,128)S(1)} %broadcast_select_fusion.2), channel_id=1, replica_groups=mesh['grp'=8,'cli'=4] {'grp','cli'}, use_global_device_ids=true, to_apply=%region_21.22 | all-reduce | flops 128 | bytes 1024 | tf_op jit(solution)/shard_map/psum | solution.py:253
  967.8 51.4 %copy.99 = bf16[4,12800,768]{2,1,0:T(8,128)(2,1)} copy(bf16[4,12800,768]{2,0,1:T(4,128)(2,1)} %all-gather.8.cloned.1.call-done) | data formatting | bytes 157286400 | tf_op jit(solution)/shard_map/while | solution.py:301
  1020.5 166.1 %while.38 = (s32[]{:T(128)}, f32[4,512]{1,0:T(4,128)S(1)}, f32[4,512]{1,0:T(4,128)S(1)}, bf16[4,512]{1,0:T(4,128)(2,1)S(1)}, bf16[4,512,768]{2,1,0:T(8,128)(2,1)...) while((s32[]{:T(128)}, f32[4,512]{1,0:T(4,128)S(1)}, ...), condition=%wide.region_14.15_spmd, body=%wide.region_11.14_spmd.sunk | while | flops 10086000640 | bytes 72927864 | solution.py:301
  1020.5 21.3 fusion.288
  1062.0 21.3 fusion.288
  1103.6 21.3 fusion.288
  1145.1 21.3 fusion.288
  1219.3 48.1 %broadcast_in_dim.238 = f32[4,12800,768]{2,1,0:T(8,128)} broadcast(f32[]{:T(128)} %constant.231.clone.1), dimensions={} | broadcast | bytes 157286400 | tf_op jit(solution)/shard_map/broadcast_in_dim | solution.py:344
  1267.4 320.8 %while.39 = (s32[]{:T(128)}, f32[4,12800,768]{2,1,0:T(8,128)}, f32[4,128,768]{2,1,0:T(8,128)}, s32[4]{0:T(128)S(1)}, s32[512]{0:T(512)S(1)}, /*index=5*/f32[512]...) while((s32[]{:T(128)}, f32[4,12800,768]{2,1,0:T(8,128)}, ...), condition=%wide.region_28.29_spmd.clone, body=%wide.region_27.28_spmd.clone.sunk | while | flops 7571046400 | bytes 207235280 | solution.py:345
  1271.2 26.9 constant_dynamic-slice_fusion.30
  1310.3 28.5 bitcast_dynamic-update-slice_fusion.2
  1351.4 26.9 constant_dynamic-slice_fusion.30
  1390.4 28.6 bitcast_dynamic-update-slice_fusion.2
  1431.6 26.9 constant_dynamic-slice_fusion.30
  1470.6 28.6 bitcast_dynamic-update-slice_fusion.2
  1511.8 26.9 constant_dynamic-slice_fusion.30
  1550.9 28.6 bitcast_dynamic-update-slice_fusion.2
  1665.7 46.9 %broadcast_select_fusion = f32[4,9344,768]{2,0,1:T(4,128)} fusion(f32[9344,768]{1,0:T(8,128)} %get-tuple-element.391, pred[4]{0:T(512)(128)(4,1)S(1)} %copy-done.60), kind=kLoop, calls=%fused_computation.140 | loop fusion | flops 28704768 | bytes 143523840 | tf_op jit(solution)/shard_map/jit(_where)/select_n | solution.py:363
  1713.2 18.4 all_gather.31
  1731.8 75.4 %scatter_fusion = f32[4,12800,768]{2,1,0:T(8,128)} fusion(f32[4,12800,768]{2,1,0:T(8,128)} %get-tuple-element.154, s32[512]{0:T(512)S(1)} %bitcast.358, f32[512,768]{1,0:T(8,128)S(1)} %convert_element_type.245), kind=kCustom, calls=%fused_computation.2 | custom fusion | flops 393216 | bytes 4722688 | tf_op jit(solution)/shard_map/scatter-add | solution.py:357
  1807.2 77.9 %convert_element_type.246 = bf16[4,12800,768]{2,1,0:T(8,128)(2,1)} convert(f32[4,12800,768]{2,1,0:T(8,128)} %scatter_fusion) | non-fusion elementwise | flops 39321600 | bytes 235929600 | tf_op jit(solution)/shard_map/convert_element_type | solution.py:361
  1887.7 39.6 %psum.38 = f32[]{:T(128)} all-reduce(f32[]{:T(128)S(6)} %div.149), channel_id=1, replica_groups=mesh['grp'=8,'cli'=4] {'grp','cli'}, use_global_device_ids=true, to_apply=%region_24.25 | all-reduce | flops 1 | bytes 8 | tf_op jit(solution)/shard_map/psum | solution.py:366
  1930.1 1468.0 %all-reduce.11.cloned.1.call-done = f32[4,9344,768]{2,0,1:T(4,128)} async-done(((f32[4,9344,768]{2,0,1:T(4,128)}), f32[4,9344,768]{2,0,1:T(4,128)}) %all-reduce.11.cloned.1.call-update) | async-done | bytes 114819088
  3406.4 432.9 %reduce-scatter.5.cloned.1.call-done = bf16[4,1600,768]{2,1,0:T(8,128)(2,1)} async-done(((bf16[4,12800,768]{2,1,0:T(8,128)(2,1)}), bf16[4,1600,768]{2,1,0:T(8,128)(2,1)}) %reduce-scatter.5.cloned.1.call-update) | async-done | bytes 9830416 | tf_op jit(solution)/shard_map/reduce_scatter | solution.py:360
  3839.3 37.0 multiply_subtract_fusion
  (463 shorter events, 412.8 us)
Async XLA Ops:
  7.2 384.9 %all-gather.8.cloned.1.call-start = ((), (), s32[]{:S(2)}) async-start(), calls=%async_computation.2 | async-start | bytes 88473600 | tf_op jit(solution)/shard_map/all_gather | solution.py:263
  36.9 668.4 %all-gather.10.cloned.1.call-start = ((), (), s32[]{:S(2)}) async-start(), calls=%async_computation.3 | async-start | bytes 59203584 | tf_op jit(solution)/shard_map/all_gather | solution.py:262
  40.9 786.7 %all-reduce.9.cloned.1.call-start = ((), (), s32[]{:S(2)}) async-start(), calls=%async_computation.8 | async-start | bytes 6291456
  414.2 606.2 %all-gather.12.cloned.1.call-start = ((), (), s32[]{:S(2)}) async-start(), calls=%async_computation.4 | async-start | bytes 3932160 | tf_op jit(solution)/shard_map/all_gather | solution.py:289
  743.8 86.4 %copy-start.6 = (f32[4,14,768]{2,0,1:T(4,128)S(1)}, f32[4,14,768]{2,0,1:T(4,128)}, u32[]{:S(2)}) copy-start(f32[4,14,768]{2,0,1:T(4,128)} %param.24) | copy-start | bytes 516100
  743.9 86.4 %copy-start.19 = (s32[1,128]{1,0:T(1,128)S(1)}, s32[1,128]{1,0:T(1,128)}, u32[]{:S(2)}) copy-start(s32[1,128]{1,0:T(1,128)} %param.18) | copy-start | bytes 1540
  830.3 113.4 %copy-start.66 = (s32[1,128]{1,0:T(1,128)S(1)}, s32[1,128]{1,0:T(1,128)}, u32[]{:S(2)}) copy-start(s32[1,128]{1,0:T(1,128)} %param.17) | copy-start | bytes 1540
  899.2 120.4 %copy-start = (f32[4,128,768]{2,1,0:T(8,128)}, f32[4,128,768]{2,1,0:T(8,128)S(1)}, u32[]{:S(2)}) copy-start(f32[4,128,768]{2,1,0:T(8,128)S(1)} %get-tuple-element.767) | copy-start | bytes 4718596
  899.2 723.1 %reduce-scatter.3.cloned.1.call-start = ((), (), s32[]{:S(2)}) async-start(), calls=%async_computation.5 | async-start | bytes 1966080 | tf_op jit(solution)/shard_map/reduce_scatter | solution.py:346
  962.7 56.5 %copy-start.25 = (s32[4,1,128]{2,1,0:T(1,128)}, s32[4,1,128]{2,1,0:T(1,128)S(1)}, u32[]{:S(2)}) copy-start(s32[4,1,128]{2,1,0:T(1,128)S(1)} %all-gather.2) | copy-start | bytes 6148
  963.4 56.2 %copy-start.17 = (f32[768]{0:T(1024)}, f32[768]{0:T(1024)S(1)}, u32[]{:S(2)}) copy-start(f32[768]{0:T(1024)S(1)} %get-tuple-element.306) | copy-start | bytes 9220
  963.4 56.2 %copy-start.21 = (f32[768]{0:T(1024)}, f32[768]{0:T(1024)S(1)}, u32[]{:S(2)}) copy-start(f32[768]{0:T(1024)S(1)} %get-tuple-element.305) | copy-start | bytes 9220
  1020.5 188.0 %copy-start.70 = (f32[4]{0:T(128)S(1)}, f32[4]{0:T(128)}, u32[]{:S(2)}) copy-start(f32[4]{0:T(128)} %fusion.185) | copy-start | bytes 52
  1020.5 188.0 %copy-start.71 = (f32[128]{0:T(128)S(1)}, f32[128]{0:T(128)}, u32[]{:S(2)}) copy-start(f32[128]{0:T(128)} %pad_maximum_fusion.3) | copy-start | bytes 1540
  1020.5 188.6 %copy-start.68 = (f32[127]{0:T(128)S(1)}, f32[127]{0:T(128)}, u32[]{:S(2)}) copy-start(f32[127]{0:T(128)} %copy-done.67) | copy-start | bytes 1528
  1020.5 198.8 %copy-start.50 = (f32[512]{0:T(512)S(1)}, f32[512]{0:T(512)}, u32[]{:S(2)}) copy-start(f32[512]{0:T(512)} %select_reduce_fusion) | copy-start | bytes 6148
  1186.6 80.8 %copy-start.27 = (pred[512]{0:T(512)(128)(4,1)}, pred[512]{0:T(512)(128)(4,1)S(1)}, u32[]{:S(2)}) copy-start(pred[512]{0:T(512)(128)(4,1)S(1)} %get-tuple-element.790) | copy-start | bytes 1540
  1219.3 48.1 %copy-start.26 = (s32[4,1,128]{2,1,0:T(1,128)S(1)}, s32[4,1,128]{2,1,0:T(1,128)}, u32[]{:S(2)}) copy-start(s32[4,1,128]{2,1,0:T(1,128)} %copy-done.25) | copy-start | bytes 6148
  1267.4 321.3 %copy-start.5 = (bf16[128,768]{1,0:T(8,128)(2,1)S(1)}, bf16[128,768]{1,0:T(8,128)(2,1)}, u32[]{:S(2)}) copy-start(bf16[128,768]{1,0:T(8,128)(2,1)} %fusion.131) | copy-start | bytes 589828
  1267.4 321.3 %copy-start.33 = (f32[768]{0:T(1024)S(1)}, f32[768]{0:T(1024)}, u32[]{:S(2)}) copy-start(f32[768]{0:T(1024)} %get-tuple-element.304) | copy-start | bytes 9220
  1271.2 28.5 copy-start.28
  1351.3 28.5 copy-start.28
  1431.6 28.5 copy-start.28
  1511.8 28.5 copy-start.28
  1588.2 340.1 %all-reduce.7.cloned.1.call-start = ((), (), s32[]{:S(2)}) async-start(), calls=%async_computation.7 | async-start | bytes 344064 | tf_op jit(solution)/shard_map/psum | solution.py:366
  1598.8 36.6 copy-start.45
  1664.8 1733.3 %all-reduce.11.cloned.1.call-start = ((), (), s32[]{:S(2)}) async-start(), calls=%async_computation.9 | async-start | bytes 229638144
  1712.6 2126.7 %reduce-scatter.5.cloned.1.call-start = ((), (), s32[]{:S(2)}) async-start(), calls=%async_computation.6 | async-start | bytes 88473600 | tf_op jit(solution)/shard_map/reduce_scatter | solution.py:360
  1885.1 42.1 %copy-start.69 = (f32[4]{0:T(128)S(1)}, f32[4]{0:T(128)}, u32[]{:S(2)}) copy-start(f32[4]{0:T(128)} %get-tuple-element.308) | copy-start | bytes 52
  1885.1 43.2 %copy-start.7 = (f32[4,14,768]{2,0,1:T(4,128)S(1)}, f32[4,14,768]{2,0,1:T(4,128)}, u32[]{:S(2)}) copy-start(f32[4,14,768]{2,0,1:T(4,128)} %param.24) | copy-start | bytes 516100
  1885.1 43.2 %copy-start.16 = (f32[4,14,768]{2,0,1:T(4,128)S(1)}, f32[4,14,768]{2,0,1:T(4,128)}, u32[]{:S(2)}) copy-start(f32[4,14,768]{2,0,1:T(4,128)} %param.25) | copy-start | bytes 516100
  3406.4 469.9 %copy-start.14 = (f32[4,14,768]{2,0,1:T(4,128)S(1)}, f32[4,14,768]{2,0,1:T(4,128)}, u32[]{:S(2)}) copy-start(f32[4,14,768]{2,0,1:T(4,128)} %all-reduce.7.cloned.1.call-done) | copy-start | bytes 516100
  (52 other events, 273.0 us)
Sparse Core Ops, SparseCore 0:
  37.1 355.0 all-gather.7
  395.5 309.8 all-gather.9
  708.3 119.2 all-reduce.8
  899.3 63.4 all-gather.11
  1588.3 33.9 reduce-scatter.2
  1664.9 121.1 all-reduce.6
  1792.5 1605.5 all-reduce.10
  3402.2 437.0 reduce-scatter.4
where the time goes:
time: 3900 us; the launch traced here: 3880 us
  waiting for transfers between devices  2630 us (67%)
  matrix products  378 us (10%)
  local copies, waits for them, and re-layouts  356 us (9%)
  other arithmetic  330 us (8%)
  blocking collectives  162 us (4%)
    unnamed x10, waiting for transfers between devices  1550 us
    reduce_scatter x1, waiting for transfers between devices, body(): lax.psum_scatter(grad_table.astype(jnp.bfloat16), 'grp', scatter_dimensio...  433 us
    all_gather x1, waiting for transfers between devices, body(): lax.all_gather(table.astype(jnp.bfloat16), 'grp', axis=1, tiled=True)  338 us
    all_gather x1, waiting for transfers between devices, body(): lax.all_gather(stack.astype(jnp.bfloat16), ('grp', 'cli'), axis=1, tiled=...  290 us
    dot_general x30, matrix products, project(): lax.dot_general(inputs, matrix, (((1,), (1,)), ((), ())), preferred_eleme...  173 us
    dot_general x8, matrix products, outer_rows(): lax.dot_general(left, right, (((0,), (0,)), ((), ())), preferred_element_...  119 us
    dynamic_slice x4, local copies, waits for them, and re-layouts, head_back(): lax.dynamic_index_in_dim(grad_table, model_pick, 0, keepdims=False)  108 us
  transfers between devices with their start and end apart: 8, of which 6 were waited for; matrix products, arithmetic and copies ran while one was open for 9% of the time, Pallas kernels for 0%

commit v1 on v0

--- a/solution.py
+++ b/solution.py
@@ -260,7 +260,23 @@
         lax.all_gather(model_column, "cli", axis=0, tiled=True),
     )
     stack_all = lax.all_gather(stack.astype(jnp.bfloat16), ("grp", "cli"), axis=1, tiled=True)
-    table_part = lax.all_gather(table.astype(jnp.bfloat16), "grp", axis=1, tiled=True)
+    value = table.astype(jnp.bfloat16)
+    ways, here, step = (lax.axis_size("grp"), lax.axis_index("grp"), value.shape[1])
+    dims = [n * ways if d == 1 else n for d, n in enumerate(value.shape)]
+    table_part = lax.dynamic_update_slice_in_dim(
+        jnp.zeros(dims, value.dtype), value, here * step, axis=1
+    )
+    going_up = going_down = value
+    for far in range(1, ways // 2 + 1):
+        going_up = lax.ppermute(going_up, "grp", [(d, (d + 1) % ways) for d in range(ways)])
+        table_part = lax.dynamic_update_slice_in_dim(
+            table_part, going_up, (here - far) % ways * step, axis=1
+        )
+        if 2 * far < ways:
+            going_down = lax.ppermute(going_down, "grp", [(d, (d - 1) % ways) for d in range(ways)])
+            table_part = lax.dynamic_update_slice_in_dim(
+                table_part, going_down, (here + far) % ways * step, axis=1
+            )
     part_rows = table_part.shape[1]
 
     def locate(global_ids):

time: 3900 us -> 4060 us (1.041)
  local copies, waits for them, and re-layouts: 356 us -> 449 us
  waiting for transfers between devices: 2630 us -> 2680 us
    ppermute x0 -> x7, waiting for transfers between devices: none -> 665 us  [the longest x4 665 us: body(): lax.ppermute(going_up, 'grp', [(d, (d + 1) % ways) for d in range(ways)])]
    reduce_scatter x1, waiting for transfers between devices: 433 us -> 0.01 us  [body(): lax.psum_scatter(grad_table.astype(jnp.bfloat16), 'grp', scatter_dimensio...]
    all_gather x1 -> x0, waiting for transfers between devices: 338 us -> none  [body(): lax.all_gather(table.astype(jnp.bfloat16), 'grp', axis=1, tiled=True)]
    unnamed x10 -> x9, waiting for transfers between devices: 1550 us -> 1810 us
    all_gather x1, waiting for transfers between devices: 290 us -> 194 us  [body(): lax.all_gather(stack.astype(jnp.bfloat16), ('grp', 'cli'), axis=1, tiled=...]
    dynamic_update_slice x0 -> x8, local copies, waits for them, and re-layouts: none -> 86.9 us  [the longest x4 36.6 us: body(): lax.dynamic_update_slice_in_dim(table_part, going_up, (here - far) % ways...]
  transfers between devices with their start and end apart: 8 -> 14, of which waited for: 6 -> 8; matrix products, arithmetic and copies ran while one was open for 9% -> 9% of each run, Pallas kernels for 0% -> 0%
where the time goes in v1:
time: 4060 us; the launch traced here: 4040 us
  waiting for transfers between devices  2680 us (66%)
  local copies, waits for them, and re-layouts  449 us (11%)
  matrix products  378 us (9%)
  other arithmetic  330 us (8%)
  blocking collectives  162 us (4%)
    unnamed x9, waiting for transfers between devices  1810 us
    ppermute x4, waiting for transfers between devices, body(): lax.ppermute(going_up, 'grp', [(d, (d + 1) % ways) for d in range(ways)])  665 us
    all_gather x1, waiting for transfers between devices, body(): lax.all_gather(stack.astype(jnp.bfloat16), ('grp', 'cli'), axis=1, tiled=...  194 us
    dot_general x30, matrix products, project(): lax.dot_general(inputs, matrix, (((1,), (1,)), ((), ())), preferred_eleme...  174 us
    dot_general x8, matrix products, outer_rows(): lax.dot_general(left, right, (((0,), (0,)), ((), ())), preferred_element_...  119 us
    dynamic_slice x4, local copies, waits for them, and re-layouts, head_back(): lax.dynamic_index_in_dim(grad_table, model_pick, 0, keepdims=False)  108 us
  transfers between devices with their start and end apart: 14, of which 8 were waited for; matrix products, arithmetic and copies ran while one was open for 9% of the time, Pallas kernels for 0%

profile of v1, /device:TPU:0, one launch (start us, length us, event | category | flops | bytes accessed | tf_op | source)
XLA Modules:
  0.0 4042.8 jit_solution(12684281686443242338)
XLA Ops:
  8.1 30.5 broadcast_in_dim.235
  38.6 26.6 constant_dynamic-update-slice_fusion.7
  68.4 209.2 %collective-permute-done = bf16[4,1600,768]{2,0,1:T(4,128)(2,1)S(1)} collective-permute-done((bf16[4,1600,768]{2,0,1:T(4,128)(2,1)S(1)}, bf16[4,1600,768]{2,0,1:T(4,128)(2,1)S(1)}, u32[]{:S(2)}, u32[]{:S(2)}) %collective-permute-start) | collective-permute-done | bytes 9830432 | tf_op jit(solution)/shard_map/ppermute | solution.py:271
  284.2 209.2 %collective-permute-done.2 = bf16[4,1600,768]{2,0,1:T(4,128)(2,1)S(1)} collective-permute-done((bf16[4,1600,768]{2,0,1:T(4,128)(2,1)S(1)}, bf16[4,1600,768]{2,0,1:T(4,128)(2,1)S(1)}, u32[]{:S(2)}, u32[]{:S(2)}) %collective-permute-start.2) | collective-permute-done | bytes 9830432 | tf_op jit(solution)/shard_map/ppermute | solution.py:271
  498.7 206.0 %collective-permute-done.4 = bf16[4,1600,768]{2,0,1:T(4,128)(2,1)} collective-permute-done((bf16[4,1600,768]{2,0,1:T(4,128)(2,1)S(1)}, bf16[4,1600,768]{2,0,1:T(4,128)(2,1)}, u32[]{:S(2)}, u32[]{:S(2)}) %collective-permute-start.4) | collective-permute-done | bytes 9830432 | tf_op jit(solution)/shard_map/ppermute | solution.py:271
  774.0 40.3 collective-permute-done.6
  851.0 202.9 %all-reduce.9.cloned.1.call-done = bf16[4,512,768]{2,0,1:T(4,128)(2,1)} async-done(((bf16[4,512,768]{2,0,1:T(4,128)(2,1)}), bf16[4,512,768]{2,0,1:T(4,128)(2,1)}) %all-reduce.9.cloned.1.call-update) | async-done | bytes 3145744
  1055.3 193.6 %all-gather.7.cloned.1.call-done = bf16[4,9344,768]{2,0,1:T(4,128)(2,1)} async-done(((bf16[4,292,768]{2,0,1:T(4,128)(2,1)}), bf16[4,9344,768]{2,0,1:T(4,128)(2,1)}) %all-gather.7.cloned.1.call-update) | async-done | bytes 57409552 | tf_op jit(solution)/shard_map/all_gather | solution.py:262
  1248.9 37.9 copy.97
  1288.1 68.9 %while.37 = (s32[]{:T(128)}, bf16[4,128,768]{2,1,0:T(8,128)(2,1)}, f32[4,128,768]{2,1,0:T(8,128)S(1)}, f32[4,14,768]{2,0,1:T(4,128)S(1)}, bf16[4,9344,768]{2,1,0...) while((s32[]{:T(128)}, bf16[4,128,768]{2,1,0:T(8,128)(2,1)}, ...), condition=%wide.region_10.11_spmd, body=%wide.region_1.10_spmd.sunk | while | flops 1896827008 | bytes 24394716 | solution.py:304
  1359.2 41.2 %psum.37 = f32[32,4]{0,1:T(4,128)S(1)} all-reduce(f32[32,4]{0,1:T(4,128)S(1)} %broadcast_select_fusion.2), channel_id=1, replica_groups=mesh['grp'=8,'cli'=4] {'grp','cli'}, use_global_device_ids=true, to_apply=%region_21.22 | all-reduce | flops 128 | bytes 1024 | tf_op jit(solution)/shard_map/psum | solution.py:253
  1424.7 51.4 %copy.99 = bf16[4,12800,768]{2,1,0:T(8,128)(2,1)} copy(bf16[4,12800,768]{2,0,1:T(4,128)(2,1)} %constant_dynamic-update-slice_fusion) | data formatting | bytes 157286400 | tf_op jit(solution)/shard_map/while | solution.py:317
  1477.4 166.1 %while.38 = (s32[]{:T(128)}, f32[4,512]{1,0:T(4,128)S(1)}, f32[4,512]{1,0:T(4,128)S(1)}, bf16[4,512]{1,0:T(4,128)(2,1)S(1)}, bf16[4,512,768]{2,1,0:T(8,128)(2,1)...) while((s32[]{:T(128)}, f32[4,512]{1,0:T(4,128)S(1)}, ...), condition=%wide.region_14.15_spmd, body=%wide.region_11.14_spmd.sunk | while | flops 10086000640 | bytes 72927864 | solution.py:317
  1477.4 21.3 fusion.288
  1518.9 21.3 fusion.288
  1560.4 21.3 fusion.288
  1676.2 48.1 %broadcast_in_dim.242 = f32[4,12800,768]{2,1,0:T(8,128)} broadcast(f32[]{:T(128)} %constant.273.clone.1), dimensions={} | broadcast | bytes 157286400 | tf_op jit(solution)/shard_map/broadcast_in_dim | solution.py:360
  1724.3 320.8 %while.39 = (s32[]{:T(128)}, f32[4,12800,768]{2,1,0:T(8,128)}, f32[4,128,768]{2,1,0:T(8,128)}, s32[4]{0:T(128)S(1)}, s32[512]{0:T(512)S(1)}, /*index=5*/f32[512]...) while((s32[]{:T(128)}, f32[4,12800,768]{2,1,0:T(8,128)}, ...), condition=%wide.region_28.29_spmd.clone, body=%wide.region_27.28_spmd.clone.sunk | while | flops 7571046400 | bytes 207235280 | solution.py:361
  1728.1 26.9 constant_dynamic-slice_fusion.30
  1767.2 28.5 bitcast_dynamic-update-slice_fusion.2
  1808.2 26.9 constant_dynamic-slice_fusion.30
  1847.3 28.6 bitcast_dynamic-update-slice_fusion.2
  1888.4 26.9 constant_dynamic-slice_fusion.30
  1927.5 28.6 bitcast_dynamic-update-slice_fusion.2
  1968.6 26.9 constant_dynamic-slice_fusion.30
  2007.7 28.6 bitcast_dynamic-update-slice_fusion.2
  2122.5 46.9 %broadcast_select_fusion = f32[4,9344,768]{2,0,1:T(4,128)} fusion(f32[9344,768]{1,0:T(8,128)} %get-tuple-element.393, pred[4]{0:T(512)(128)(4,1)S(1)} %copy-done.64), kind=kLoop, calls=%fused_computation.140 | loop fusion | flops 28704768 | bytes 143523840 | tf_op jit(solution)/shard_map/jit(_where)/select_n | solution.py:379
  2188.4 75.4 %scatter_fusion = f32[4,12800,768]{2,1,0:T(8,128)} fusion(f32[4,12800,768]{2,1,0:T(8,128)} %get-tuple-element.154, s32[512]{0:T(512)S(1)} %bitcast.358, f32[512,768]{1,0:T(8,128)S(1)} %convert_element_type.245), kind=kCustom, calls=%fused_computation.2 | custom fusion | flops 393216 | bytes 4722688 | tf_op jit(solution)/shard_map/scatter-add | solution.py:373
  2263.9 78.0 %convert_element_type.246 = bf16[4,12800,768]{2,1,0:T(8,128)(2,1)} convert(f32[4,12800,768]{2,1,0:T(8,128)} %scatter_fusion) | non-fusion elementwise | flops 39321600 | bytes 235929600 | tf_op jit(solution)/shard_map/convert_element_type | solution.py:377
  2344.4 39.1 psum.38
  2386.6 1602.7 %all-reduce.11.cloned.1.call-done = f32[4,9344,768]{2,0,1:T(4,128)} async-done(((f32[4,9344,768]{2,0,1:T(4,128)}), f32[4,9344,768]{2,0,1:T(4,128)}) %all-reduce.11.cloned.1.call-update) | async-done | bytes 114819088
  3997.5 37.0 multiply_subtract_fusion
  (504 shorter events, 550.4 us)
Async XLA Ops:
  8.0 1045.8 %all-reduce.9.cloned.1.call-start = ((), (), s32[]{:S(2)}) async-start(), calls=%async_computation.7 | async-start | bytes 6291456
  38.6 669.5 %copy-start.69 = (s32[1,128]{1,0:T(1,128)S(1)}, s32[1,128]{1,0:T(1,128)}, u32[]{:S(2)}) copy-start(s32[1,128]{1,0:T(1,128)} %param.16) | copy-start | bytes 1540
  65.2 212.5 %collective-permute-start = (bf16[4,1600,768]{2,0,1:T(4,128)(2,1)S(1)}, bf16[4,1600,768]{2,0,1:T(4,128)(2,1)S(1)}, u32[]{:S(2)}, u32[]{:S(2)}) collective-permute-start(bf16[4,1600,768]{2,0,1:T(4,128)(2,1)S(1)} %get-tuple-element.386), channel_id=1, source_target_pairs={{0,4},{4,8},{8,12},{12,16},{16,20},{20,24},{24,28},{28,0},{1,5},{5... | collective-permute-start | bytes 29491208 | tf_op jit(solution)/shard_map/ppermute | solution.py:271
  65.6 216.7 %collective-permute-start.1 = (bf16[4,1600,768]{2,0,1:T(4,128)(2,1)S(1)}, bf16[4,1600,768]{2,0,1:T(4,128)(2,1)S(1)}, u32[]{:S(2)}, u32[]{:S(2)}) collective-permute-start(bf16[4,1600,768]{2,0,1:T(4,128)(2,1)S(1)} %get-tuple-element.386), channel_id=1, source_target_pairs={{0,28},{4,0},{8,4},{12,8},{16,12},{20,16},{24,20},{28,24},{1,29},{... | collective-permute-start | bytes 29491208 | tf_op jit(solution)/shard_map/ppermute | solution.py:276
  281.5 211.8 %collective-permute-start.2 = (bf16[4,1600,768]{2,0,1:T(4,128)(2,1)S(1)}, bf16[4,1600,768]{2,0,1:T(4,128)(2,1)S(1)}, u32[]{:S(2)}, u32[]{:S(2)}) collective-permute-start(bf16[4,1600,768]{2,0,1:T(4,128)(2,1)S(1)} %collective-permute-done), channel_id=1, source_target_pairs={{0,4},{4,8},{8,12},{12,16},{16,20},{20,24},{24,28},{28,0},{1,5},{5... | collective-permute-start | bytes 29491208 | tf_op jit(solution)/shard_map/ppermute | solution.py:271
  282.3 211.1 %copy-start.5 = (bf16[4,1600,768]{2,0,1:T(4,128)(2,1)}, bf16[4,1600,768]{2,0,1:T(4,128)(2,1)S(1)}, u32[]{:S(2)}) copy-start(bf16[4,1600,768]{2,0,1:T(4,128)(2,1)S(1)} %collective-permute-done.1) | copy-start | bytes 29491204
  282.3 213.6 %collective-permute-start.3 = (bf16[4,1600,768]{2,0,1:T(4,128)(2,1)S(1)}, bf16[4,1600,768]{2,0,1:T(4,128)(2,1)}, u32[]{:S(2)}, u32[]{:S(2)}) collective-permute-start(bf16[4,1600,768]{2,0,1:T(4,128)(2,1)S(1)} %collective-permute-done.1), channel_id=1, source_target_pairs={{0,28},{4,0},{8,4},{12,8},{16,12},{20,16},{24,20},{28,24},{1,29},{... | collective-permute-start | bytes 29491208 | tf_op jit(solution)/shard_map/ppermute | solution.py:276
  493.4 211.4 %collective-permute-start.4 = (bf16[4,1600,768]{2,0,1:T(4,128)(2,1)S(1)}, bf16[4,1600,768]{2,0,1:T(4,128)(2,1)}, u32[]{:S(2)}, u32[]{:S(2)}) collective-permute-start(bf16[4,1600,768]{2,0,1:T(4,128)(2,1)S(1)} %collective-permute-done.2), channel_id=1, source_target_pairs={{0,4},{4,8},{8,12},{12,16},{16,20},{20,24},{24,28},{28,0},{1,5},{5... | collective-permute-start | bytes 29491208 | tf_op jit(solution)/shard_map/ppermute | solution.py:271
  497.2 267.6 %collective-permute-start.5 = (bf16[4,1600,768]{2,0,1:T(4,128)(2,1)}, bf16[4,1600,768]{2,0,1:T(4,128)(2,1)}, u32[]{:S(2)}, u32[]{:S(2)}) collective-permute-start(bf16[4,1600,768]{2,0,1:T(4,128)(2,1)} %collective-permute-done.3), channel_id=1, source_target_pairs={{0,28},{4,0},{8,4},{12,8},{16,12},{20,16},{24,20},{28,24},{1,29},{... | collective-permute-start | bytes 29491208 | tf_op jit(solution)/shard_map/ppermute | solution.py:276
  704.8 109.5 %collective-permute-start.6 = (bf16[4,1600,768]{2,0,1:T(4,128)(2,1)}, bf16[4,1600,768]{2,0,1:T(4,128)(2,1)}, u32[]{:S(2)}, u32[]{:S(2)}) collective-permute-start(bf16[4,1600,768]{2,0,1:T(4,128)(2,1)} %collective-permute-done.4), channel_id=1, source_target_pairs={{0,4},{4,8},{8,12},{12,16},{16,20},{20,24},{24,28},{28,0},{1,5},{5... | collective-permute-start | bytes 29491208 | tf_op jit(solution)/shard_map/ppermute | solution.py:271
  845.6 403.3 %all-gather.7.cloned.1.call-start = ((), (), s32[]{:S(2)}) async-start(), calls=%async_computation.2 | async-start | bytes 59203584 | tf_op jit(solution)/shard_map/all_gather | solution.py:262
  849.5 627.8 %all-gather.9.cloned.1.call-start = ((), (), s32[]{:S(2)}) async-start(), calls=%async_computation.3 | async-start | bytes 3932160 | tf_op jit(solution)/shard_map/all_gather | solution.py:305
  1055.3 232.8 %copy-start.10 = (f32[4,14,768]{2,0,1:T(4,128)S(1)}, f32[4,14,768]{2,0,1:T(4,128)}, u32[]{:S(2)}) copy-start(f32[4,14,768]{2,0,1:T(4,128)} %param.24) | copy-start | bytes 516100
  1055.3 232.8 %copy-start.23 = (s32[1,128]{1,0:T(1,128)S(1)}, s32[1,128]{1,0:T(1,128)}, u32[]{:S(2)}) copy-start(s32[1,128]{1,0:T(1,128)} %param.18) | copy-start | bytes 1540
  1288.1 112.4 %copy-start.70 = (s32[1,128]{1,0:T(1,128)S(1)}, s32[1,128]{1,0:T(1,128)}, u32[]{:S(2)}) copy-start(s32[1,128]{1,0:T(1,128)} %param.17) | copy-start | bytes 1540
  1357.0 119.5 %copy-start = (f32[4,128,768]{2,1,0:T(8,128)}, f32[4,128,768]{2,1,0:T(8,128)S(1)}, u32[]{:S(2)}) copy-start(f32[4,128,768]{2,1,0:T(8,128)S(1)} %get-tuple-element.768) | copy-start | bytes 4718596
  1357.0 722.1 %reduce-scatter.3.cloned.1.call-start = ((), (), s32[]{:S(2)}) async-start(), calls=%async_computation.4 | async-start | bytes 1966080 | tf_op jit(solution)/shard_map/reduce_scatter | solution.py:362
  1419.6 56.5 %copy-start.29 = (s32[4,1,128]{2,1,0:T(1,128)}, s32[4,1,128]{2,1,0:T(1,128)S(1)}, u32[]{:S(2)}) copy-start(s32[4,1,128]{2,1,0:T(1,128)S(1)} %all-gather.2) | copy-start | bytes 6148
  1420.3 56.2 %copy-start.21 = (f32[768]{0:T(1024)}, f32[768]{0:T(1024)S(1)}, u32[]{:S(2)}) copy-start(f32[768]{0:T(1024)S(1)} %get-tuple-element.306) | copy-start | bytes 9220
  1420.3 56.2 %copy-start.25 = (f32[768]{0:T(1024)}, f32[768]{0:T(1024)S(1)}, u32[]{:S(2)}) copy-start(f32[768]{0:T(1024)S(1)} %get-tuple-element.305) | copy-start | bytes 9220
  1477.3 188.0 %copy-start.74 = (f32[4]{0:T(128)S(1)}, f32[4]{0:T(128)}, u32[]{:S(2)}) copy-start(f32[4]{0:T(128)} %fusion.185) | copy-start | bytes 52
  1477.3 188.0 %copy-start.75 = (f32[128]{0:T(128)S(1)}, f32[128]{0:T(128)}, u32[]{:S(2)}) copy-start(f32[128]{0:T(128)} %pad_maximum_fusion.3) | copy-start | bytes 1540
  1477.3 188.6 %copy-start.72 = (f32[127]{0:T(128)S(1)}, f32[127]{0:T(128)}, u32[]{:S(2)}) copy-start(f32[127]{0:T(128)} %copy-done.71) | copy-start | bytes 1528
  1477.3 198.8 %copy-start.54 = (f32[512]{0:T(512)S(1)}, f32[512]{0:T(512)}, u32[]{:S(2)}) copy-start(f32[512]{0:T(512)} %select_reduce_fusion) | copy-start | bytes 6148
  1643.4 80.8 %copy-start.31 = (pred[512]{0:T(512)(128)(4,1)}, pred[512]{0:T(512)(128)(4,1)S(1)}, u32[]{:S(2)}) copy-start(pred[512]{0:T(512)(128)(4,1)S(1)} %get-tuple-element.797) | copy-start | bytes 1540
  1676.1 48.1 %copy-start.30 = (s32[4,1,128]{2,1,0:T(1,128)S(1)}, s32[4,1,128]{2,1,0:T(1,128)}, u32[]{:S(2)}) copy-start(s32[4,1,128]{2,1,0:T(1,128)} %copy-done.29) | copy-start | bytes 6148
  1724.3 321.3 %copy-start.9 = (bf16[128,768]{1,0:T(8,128)(2,1)S(1)}, bf16[128,768]{1,0:T(8,128)(2,1)}, u32[]{:S(2)}) copy-start(bf16[128,768]{1,0:T(8,128)(2,1)} %fusion.131) | copy-start | bytes 589828
  1724.3 321.3 %copy-start.37 = (f32[768]{0:T(1024)S(1)}, f32[768]{0:T(1024)}, u32[]{:S(2)}) copy-start(f32[768]{0:T(1024)} %get-tuple-element.304) | copy-start | bytes 9220
  1724.3 323.3 %copy-start.36 = (f32[768]{0:T(1024)S(1)}, f32[768]{0:T(1024)}, u32[]{:S(2)}) copy-start(f32[768]{0:T(1024)} %get-tuple-element.303) | copy-start | bytes 9220
  2045.1 339.6 %all-reduce.7.cloned.1.call-start = ((), (), s32[]{:S(2)}) async-start(), calls=%async_computation.6 | async-start | bytes 344064 | tf_op jit(solution)/shard_map/psum | solution.py:382
  2121.6 1867.6 %all-reduce.11.cloned.1.call-start = ((), (), s32[]{:S(2)}) async-start(), calls=%async_computation.8 | async-start | bytes 229638144
  2169.4 1828.1 %reduce-scatter.5.cloned.1.call-start = ((), (), s32[]{:S(2)}) async-start(), calls=%async_computation.5 | async-start | bytes 88473600 | tf_op jit(solution)/shard_map/reduce_scatter | solution.py:376
  (68 other events, 720.2 us)
Sparse Core Ops, SparseCore 0:
  845.7 208.1 all-reduce.8
  1357.1 62.5 all-gather.8
  2045.2 33.9 reduce-scatter.2
  2342.0 560.1 reduce-scatter.4
Sparse Core Ops, SparseCore 1:
  849.6 399.3 all-gather.6
  2121.7 121.0 all-reduce.6
  2250.2 1739.0 all-reduce.10
